TPU v7x, 512 devices: a whole 4x4x16 slice. The times are simulated.
512 devices in a mesh: section: 32 (over z_hi, x, y), expert: 16 (over z_lo, core).
Axes of the slice: x: 4, y: 4, z: 16 (z_hi: 2, z_lo: 8; z = z_hi * 8 + z_lo), core: 2. Of those that a mesh axis runs over, the one named last changes fastest.
Arguments:
- act_rows: bfloat16 [32, 2048, 2048], P('section', 'expert'), may hold values from -6 to 6
- cot_rows: bfloat16 [32, 2048, 2048], P('section', 'expert'), may hold values from -2.390625 to 2.390625
- expert_ids: int32 [32, 2048, 1], P('section', 'expert'), may hold values from 0 to 15; in each aligned block of 128 rows (0 to 127, 128 to 255, ..., all dimensions but the last counted through in order) at most 16 rows name the same one
- w_gate: bfloat16 [32, 16, 2048, 128], P('section', 'expert'), may hold values from -0.125 to 0.125
- w_up: bfloat16 [32, 16, 2048, 128], P('section', 'expert'), may hold values from -0.125 to 0.125
- w_down: bfloat16 [32, 16, 128, 2048], P('section', 'expert'), may hold values from -0.375 to 0.375
Outputs:
- act_grad: bfloat16 [32, 2048, 2048], P('section', 'expert')
- gate_grad: bfloat16 [32, 16, 2048, 128], P('section', 'expert')
- up_grad: bfloat16 [32, 16, 2048, 128], P('section', 'expert')
- down_grad: bfloat16 [32, 16, 128, 2048], P('section', 'expert')
Inputs may be any that keep to these rules, and one draw needn't show every extreme that they name: `expert_ids`: within the 128 rows of one device no expert is named by more than 16 rows, a bound that some block reaches; every expert serves rows somewhere.
All inputs are finite; a program needn't handle non-finite values.
Results may differ from a plain program's by a relative error of at most 0.0049.
Values may be sent and summed in bfloat16 or wider, within the bound.
No kernel may reach another device: no remote copies, remote signals or barrier semaphores. Data moves between devices by JAX's collectives and lax.ppermute only.
A program may use at most 64 MiB of HBM per device.

v0:
```python
import jax
import jax.numpy as jnp
from jax import lax
from jax.sharding import PartitionSpec as P


def passed_along(value, axis, by):
    peers = lax.axis_size(axis)
    return lax.ppermute(value, axis, [(i, (i + by) % peers) for i in range(peers)])


def joined_halves(own_part, other_part, is_upper, axis_num):
    first_half = jnp.where(is_upper, other_part, own_part)
    second_half = jnp.where(is_upper, own_part, other_part)
    return jnp.concatenate([first_half, second_half], axis=axis_num)


def slot_work(flat_rows, width, gate_full, up_full, down_full):
    act_buf = flat_rows[:, :width]
    cot_buf = flat_rows[:, width:]
    gate_pre = jnp.dot(act_buf, gate_full, preferred_element_type=jnp.float32)
    up_pre = jnp.dot(act_buf, up_full, preferred_element_type=jnp.float32)
    sigma = jax.nn.sigmoid(gate_pre)
    activ = gate_pre * sigma
    hidden = (activ * up_pre).astype(jnp.bfloat16)
    hidden_grad = lax.dot_general(
        cot_buf, down_full, (((1,), (1,)), ((), ())), preferred_element_type=jnp.float32
    )
    gate_delta = (hidden_grad * up_pre * sigma * (1.0 + gate_pre * (1.0 - sigma))).astype(
        jnp.bfloat16
    )
    up_delta = (hidden_grad * activ).astype(jnp.bfloat16)
    back_wide = lax.dot_general(
        gate_delta, gate_full, (((1,), (1,)), ((), ())), preferred_element_type=jnp.float32
    ) + lax.dot_general(
        up_delta, up_full, (((1,), (1,)), ((), ())), preferred_element_type=jnp.float32
    )
    return (back_wide, hidden, gate_delta, up_delta)


def row_work(flat_rows, width, weights):
    back_wide, hidden, gate_delta, up_delta = slot_work(
        flat_rows, width, weights[0], weights[1], weights[2]
    )
    return (back_wide.astype(jnp.bfloat16), flat_rows, hidden, gate_delta, up_delta, 1)


def per_device(act_rows, cot_rows, expert_ids, w_gate, w_up, w_down):
    n_experts = lax.axis_size("expert")
    half_count = lax.axis_size("section") // 2
    row_count = act_rows.shape[1]
    width = act_rows.shape[2]
    half_units = w_gate.shape[3]
    capacity = 2 * row_count // n_experts
    is_upper = lax.axis_index("section") >= half_count
    own_weights = (w_gate[0, 0], w_up[0, 0], w_down[0, 0])
    other_weights = passed_along(
        (own_weights[0], own_weights[1], own_weights[2]), "section", half_count
    )
    weights = (
        joined_halves(own_weights[0], other_weights[0], is_upper, 1),
        joined_halves(own_weights[1], other_weights[1], is_upper, 1),
        joined_halves(own_weights[2], other_weights[2], is_upper, 0),
    )
    route_ids = expert_ids[0, :, 0]
    onehot = (route_ids[:, None] == jnp.arange(n_experts, dtype=jnp.int32)[None, :]).astype(
        jnp.int32
    )
    ranks = jnp.cumsum(onehot, axis=0) - onehot
    slots = jnp.sum(ranks * onehot, axis=1)
    places = route_ids * capacity + slots
    packed = jnp.concatenate([act_rows[0], cot_rows[0]], axis=1)
    send_buf = jnp.zeros((n_experts * capacity, 2 * width), jnp.bfloat16).at[places].set(packed)
    send_buf = send_buf.reshape(n_experts, capacity, 2 * width)
    received = lax.all_to_all(send_buf, "expert", split_axis=0, concat_axis=0, tiled=True)
    act_back, used_rows, hidden, gate_delta, up_delta, copies = row_work(
        received.reshape(-1, 2 * width), width, weights
    )
    returned = lax.all_to_all(
        act_back.reshape(n_experts, capacity, width),
        "expert",
        split_axis=0,
        concat_axis=0,
        tiled=True,
    )
    act_grad = returned.reshape(-1, width)[places]
    act_buf = used_rows[:, :width]
    cot_buf = used_rows[:, width:]
    contract = (((0,), (0,)), ((), ()))
    gate_part = lax.dot_general(act_buf, gate_delta, contract, preferred_element_type=jnp.float32)
    up_part = lax.dot_general(act_buf, up_delta, contract, preferred_element_type=jnp.float32)
    down_part = lax.dot_general(hidden, cot_buf, contract, preferred_element_type=jnp.float32)
    own_start = is_upper.astype(jnp.int32) * half_units
    partner = passed_along((gate_part, up_part, down_part), "section", half_count)
    gate_total = lax.dynamic_slice_in_dim(gate_part + partner[0], own_start, half_units, 1)
    up_total = lax.dynamic_slice_in_dim(up_part + partner[1], own_start, half_units, 1)
    down_total = lax.dynamic_slice_in_dim(down_part + partner[2], own_start, half_units, 0)
    return (
        act_grad[None],
        gate_total.astype(jnp.bfloat16)[None, None],
        up_total.astype(jnp.bfloat16)[None, None],
        down_total.astype(jnp.bfloat16)[None, None],
    )


def solution(mesh):
    placed = (
        P("section", "expert", None),
        P("section", "expert", None),
        P("section", "expert", None),
        P("section", "expert", None, None),
        P("section", "expert", None, None),
        P("section", "expert", None, None),
    )
    return jax.shard_map(
        per_device,
        mesh=mesh,
        in_specs=placed,
        out_specs=(
            P("section", "expert", None),
            P("section", "expert", None, None),
            P("section", "expert", None, None),
            P("section", "expert", None, None),
        ),
        check_vma=False,
    )
```

profile of v0, /device:TPU:158, one launch (start us, length us, event | category | flops | bytes accessed | tf_op | source)
XLA Modules:
  0.0 851.4 jit_solution(14708987953605943925)
XLA Ops:
  0.6 0.7 fusion.29
  1.5 0.8 select_reduce_fusion
  2.4 0.7 fusion.31
  3.0 4.3 scatter_custom_fusion
  7.4 11.4 %all-to-all-start = ((bf16[16,16,4096]{2,1,0:T(8,128)(2,1)}), bf16[16,16,4096]{2,1,0:T(8,128)(2,1)S(1)}, u32[]{:S(2)}, u32[]{:S(2)}) async-start(bf16[16,16,4096]{2,1,0:T(8,128)(2,1)} %bitcast.42), calls=%async_computation | async-start | bytes 4194304 | tf_op jit(solution)/shard_map/all_to_all | solution.py:75
  18.8 8.2 collective-permute-start.2
  27.0 6.3 collective-permute-start.1
  33.4 8.2 collective-permute-start
  41.6 139.7 %collective-permute-done.2 = bf16[2048,128]{1,0:T(8,128)(2,1)} collective-permute-done((bf16[2048,128]{1,0:T(8,128)(2,1)S(1)}, bf16[2048,128]{1,0:T(8,128)(2,1)}, u32[]{:S(2)}, u32[]{:S(2)}) %collective-permute-start.2) | collective-permute-done | bytes 524320 | tf_op jit(solution)/shard_map/ppermute | solution.py:9
  181.3 1.3 broadcast_select_fusion.1
  182.6 17.5 %collective-permute-done.1 = bf16[2048,128]{1,0:T(8,128)(2,1)} collective-permute-done((bf16[2048,128]{1,0:T(8,128)(2,1)}, bf16[2048,128]{1,0:T(8,128)(2,1)}, u32[]{:S(2)}, u32[]{:S(2)}) %collective-permute-start.1) | collective-permute-done | bytes 524320 | tf_op jit(solution)/shard_map/ppermute | solution.py:9
  200.1 2.2 broadcast_select_fusion.3
  202.3 16.2 %collective-permute-done = bf16[128,2048]{1,0:T(8,128)(2,1)} collective-permute-done((bf16[128,2048]{1,0:T(8,128)(2,1)}, bf16[128,2048]{1,0:T(8,128)(2,1)}, u32[]{:S(2)}, u32[]{:S(2)}) %collective-permute-start) | collective-permute-done | bytes 524320 | tf_op jit(solution)/shard_map/ppermute | solution.py:9
  218.6 2.2 broadcast_select_fusion.5
  220.8 24.6 %all-to-all-done = bf16[16,16,4096]{2,1,0:T(8,128)(2,1)S(1)} async-done(((bf16[16,16,4096]{2,1,0:T(8,128)(2,1)}), bf16[16,16,4096]{2,1,0:T(8,128)(2,1)S(1)}, u32[]{:S(2)}, u32[]{:S(2)}) %all-to-all-start) | async-done | bytes 2097184 | tf_op jit(solution)/shard_map/all_to_all | solution.py:75
  245.9 0.6 copy-done
  247.2 0.6 multiply_convert_fusion.2
  248.3 1.5 fusion
  249.8 10.7 %all-to-all-start.1 = ((bf16[16,16,2048]{2,1,0:T(8,128)(2,1)}), bf16[16,16,2048]{2,1,0:T(8,128)(2,1)S(1)}, u32[]{:S(2)}, u32[]{:S(2)}) async-start(bf16[16,16,2048]{2,1,0:T(8,128)(2,1)} %bitcast.43), calls=%async_computation.1 | async-start | bytes 2097152 | tf_op jit(solution)/shard_map/all_to_all | solution.py:79
  260.4 1.8 fusion.21
  262.2 6.5 collective-permute-start.3
  268.7 1.8 fusion.19
  270.5 8.2 collective-permute-start.4
  278.8 1.9 fusion.13
  280.6 6.3 collective-permute-start.5
  287.0 428.4 %collective-permute-done.3 = f32[2048,256]{1,0:T(8,128)} collective-permute-done((f32[2048,256]{1,0:T(8,128)}, f32[2048,256]{1,0:T(8,128)}, u32[]{:S(2)}, u32[]{:S(2)}) %collective-permute-start.3) | collective-permute-done | bytes 2097184 | tf_op jit(solution)/shard_map/ppermute | solution.py:9
  715.4 2.4 fusion.25
  717.9 85.3 %collective-permute-done.4 = f32[2048,256]{1,0:T(8,128)} collective-permute-done((f32[2048,256]{1,0:T(8,128)}, f32[2048,256]{1,0:T(8,128)}, u32[]{:S(2)}, u32[]{:S(2)}) %collective-permute-start.4) | collective-permute-done | bytes 2097184 | tf_op jit(solution)/shard_map/ppermute | solution.py:9
  803.2 2.4 fusion.26
  805.6 41.9 %collective-permute-done.5 = f32[256,2048]{1,0:T(8,128)S(1)} collective-permute-done((f32[256,2048]{1,0:T(8,128)}, f32[256,2048]{1,0:T(8,128)S(1)}, u32[]{:S(2)}, u32[]{:S(2)}) %collective-permute-start.5) | collective-permute-done | bytes 2097184 | tf_op jit(solution)/shard_map/ppermute | solution.py:9
  847.5 2.1 fusion.27
  849.6 1.7 gather_fusion
  (23 shorter events, 1.9 us)
Async XLA Ops:
  7.4 11.4 %copy-start.2 = (bf16[1,1,2048,128]{3,2,1,0:T(8,128)(2,1)S(1)}, bf16[1,1,2048,128]{3,2,1,0:T(8,128)(2,1)}, u32[]{:S(2)}) copy-start(bf16[1,1,2048,128]{3,2,1,0:T(8,128)(2,1)} %param.9) | copy-start | bytes 1572868
  7.4 238.0 %all-to-all-start = ((bf16[16,16,4096]{2,1,0:T(8,128)(2,1)}), bf16[16,16,4096]{2,1,0:T(8,128)(2,1)S(1)}, u32[]{:S(2)}, u32[]{:S(2)}) async-start(bf16[16,16,4096]{2,1,0:T(8,128)(2,1)} %bitcast.42), calls=%async_computation | async-start | bytes 4194304 | tf_op jit(solution)/shard_map/all_to_all | solution.py:75
  18.8 162.6 %collective-permute-start.2 = (bf16[2048,128]{1,0:T(8,128)(2,1)S(1)}, bf16[2048,128]{1,0:T(8,128)(2,1)}, u32[]{:S(2)}, u32[]{:S(2)}) collective-permute-start(bf16[2048,128]{1,0:T(8,128)(2,1)S(1)} %bitcast.44), channel_id=1, source_target_pairs={{0,256},{16,272},{32,288},{48,304},{64,320},{80,336},{96,352},{112... | collective-permute-start | bytes 1572872 | tf_op jit(solution)/shard_map/ppermute | solution.py:9
  27.0 173.1 %collective-permute-start.1 = (bf16[2048,128]{1,0:T(8,128)(2,1)}, bf16[2048,128]{1,0:T(8,128)(2,1)}, u32[]{:S(2)}, u32[]{:S(2)}) collective-permute-start(bf16[2048,128]{1,0:T(8,128)(2,1)} %bitcast.9), channel_id=1, source_target_pairs={{0,256},{16,272},{32,288},{48,304},{64,320},{80,336},{96,352},{112... | collective-permute-start | bytes 1572872 | tf_op jit(solution)/shard_map/ppermute | solution.py:9
  33.4 185.2 %collective-permute-start = (bf16[128,2048]{1,0:T(8,128)(2,1)}, bf16[128,2048]{1,0:T(8,128)(2,1)}, u32[]{:S(2)}, u32[]{:S(2)}) collective-permute-start(bf16[128,2048]{1,0:T(8,128)(2,1)} %bitcast.8), channel_id=1, source_target_pairs={{0,256},{16,272},{32,288},{48,304},{64,320},{80,336},{96,352},{112... | collective-permute-start | bytes 1572872 | tf_op jit(solution)/shard_map/ppermute | solution.py:9
  245.4 1.0 copy-start
  245.4 1.2 copy-start.1
  245.8 2.0 copy-start.5
  245.8 1.2 copy-start.3
  245.9 1.4 copy-start.4
  247.0 0.8 copy-start.7
  249.8 599.9 %all-to-all-start.1 = ((bf16[16,16,2048]{2,1,0:T(8,128)(2,1)}), bf16[16,16,2048]{2,1,0:T(8,128)(2,1)S(1)}, u32[]{:S(2)}, u32[]{:S(2)}) async-start(bf16[16,16,2048]{2,1,0:T(8,128)(2,1)} %bitcast.43), calls=%async_computation.1 | async-start | bytes 2097152 | tf_op jit(solution)/shard_map/all_to_all | solution.py:79
  262.2 16.5 %copy-start.6 = (f32[256,256]{1,0:T(8,128)S(1)}, f32[256,256]{1,0:T(8,128)}, u32[]{:S(2)}) copy-start(f32[256,256]{1,0:T(8,128)} %copy-done.5) | copy-start | bytes 786436
  262.2 16.5 %copy-start.8 = (f32[256,256]{1,0:T(8,128)S(1)}, f32[256,256]{1,0:T(8,128)}, u32[]{:S(2)}) copy-start(f32[256,256]{1,0:T(8,128)} %copy-done.7) | copy-start | bytes 786436
  262.2 453.2 %collective-permute-start.3 = (f32[2048,256]{1,0:T(8,128)}, f32[2048,256]{1,0:T(8,128)}, u32[]{:S(2)}, u32[]{:S(2)}) collective-permute-start(f32[2048,256]{1,0:T(8,128)} %fusion.21), channel_id=1, source_target_pairs={{0,256},{16,272},{32,288},{48,304},{64,320},{80,336},{96,352},{112... | collective-permute-start | bytes 6291464 | tf_op jit(solution)/shard_map/ppermute | solution.py:9
  270.5 532.6 %collective-permute-start.4 = (f32[2048,256]{1,0:T(8,128)}, f32[2048,256]{1,0:T(8,128)}, u32[]{:S(2)}, u32[]{:S(2)}) collective-permute-start(f32[2048,256]{1,0:T(8,128)} %fusion.19), channel_id=1, source_target_pairs={{0,256},{16,272},{32,288},{48,304},{64,320},{80,336},{96,352},{112... | collective-permute-start | bytes 6291464 | tf_op jit(solution)/shard_map/ppermute | solution.py:9
  280.6 566.8 %collective-permute-start.5 = (f32[256,2048]{1,0:T(8,128)}, f32[256,2048]{1,0:T(8,128)S(1)}, u32[]{:S(2)}, u32[]{:S(2)}) collective-permute-start(f32[256,2048]{1,0:T(8,128)} %fusion.13), channel_id=1, source_target_pairs={{0,256},{16,272},{32,288},{48,304},{64,320},{80,336},{96,352},{112... | collective-permute-start | bytes 6291464 | tf_op jit(solution)/shard_map/ppermute | solution.py:9
where the time goes:
time: 852 us; the launch traced here: 851 us
  waiting for transfers between devices  754 us (88%)
  starting transfers between devices  65.9 us (8%)
  other arithmetic  19.5 us (2%)
  matrix products  8.91 us (1%)
    ppermute x6, waiting for transfers between devices, passed_along(): lax.ppermute(value, axis, [(i, (i + by) % peers) for i in range(peers)])  729 us
    ppermute x6, starting transfers between devices, passed_along(): lax.ppermute(value, axis, [(i, (i + by) % peers) for i in range(peers)])  43.8 us
    all_to_all x1, waiting for transfers between devices, per_device(): lax.all_to_all(send_buf, 'expert', split_axis=0, concat_axis=0, tiled=True)  24.6 us
  transfers between devices with their start and end apart: 8, of which 7 were waited for; matrix products, arithmetic and copies ran while one was open for 2% of the time, Pallas kernels for 0%

commit v1 on v0

v1 whole, which is shorter than its diff:
```python
import jax
import jax.numpy as jnp
from jax import lax
from jax.sharding import Mesh, PartitionSpec as P

PAIR = ("half", "expert")


def per_device(act_rows, cot_rows, expert_ids, w_gate, w_up, w_down):
    n_experts = lax.axis_size("expert")
    n_halves = lax.axis_size("half")
    peers = n_halves * n_experts
    row_count = act_rows.shape[1]
    width = act_rows.shape[2]
    capacity = 2 * row_count // n_experts
    gate_w, up_w, down_w = w_gate[0, 0], w_up[0, 0], w_down[0, 0]
    f32 = jnp.float32

    route_ids = expert_ids[0, :, 0]
    onehot = (route_ids[:, None] == jnp.arange(n_experts, dtype=jnp.int32)[None, :]).astype(
        jnp.int32
    )
    ranks = jnp.cumsum(onehot, axis=0) - onehot
    places = route_ids * capacity + jnp.sum(ranks * onehot, axis=1)

    slots = jnp.arange(peers * capacity, dtype=jnp.int32) % (n_experts * capacity)
    pick = (slots[:, None] == places[None, :]).astype(jnp.bfloat16)
    packed = jnp.concatenate([act_rows[0], cot_rows[0]], axis=1)
    send = jnp.dot(pick, packed, preferred_element_type=f32).astype(jnp.bfloat16)
    received = lax.all_to_all(
        send.reshape(peers, capacity, 2 * width), PAIR, split_axis=0, concat_axis=0, tiled=True
    ).reshape(-1, 2 * width)
    act_buf = received[:, :width]
    cot_buf = received[:, width:]

    gate_pre = jnp.dot(act_buf, gate_w, preferred_element_type=f32)
    up_pre = jnp.dot(act_buf, up_w, preferred_element_type=f32)
    last = (((1,), (1,)), ((), ()))
    hidden_grad = lax.dot_general(cot_buf, down_w, last, preferred_element_type=f32)
    sigma = jax.nn.sigmoid(gate_pre)
    activ = gate_pre * sigma
    hidden = (activ * up_pre).astype(jnp.bfloat16)
    gate_delta = (hidden_grad * up_pre * sigma * (1.0 + gate_pre * (1.0 - sigma))).astype(
        jnp.bfloat16
    )
    up_delta = (hidden_grad * activ).astype(jnp.bfloat16)
    back = (
        lax.dot_general(gate_delta, gate_w, last, preferred_element_type=f32)
        + lax.dot_general(up_delta, up_w, last, preferred_element_type=f32)
    ).astype(jnp.bfloat16)
    returned = lax.all_to_all(
        back.reshape(peers, capacity, width), PAIR, split_axis=0, concat_axis=0, tiled=True
    ).reshape(-1, width)
    act_grad = lax.dot_general(
        pick, returned, (((0,), (0,)), ((), ())), preferred_element_type=f32
    ).astype(jnp.bfloat16)

    rows = (((0,), (0,)), ((), ()))
    gate_grad = lax.dot_general(act_buf, gate_delta, rows, preferred_element_type=f32)
    up_grad = lax.dot_general(act_buf, up_delta, rows, preferred_element_type=f32)
    down_grad = lax.dot_general(hidden, cot_buf, rows, preferred_element_type=f32)
    return (
        act_grad[None],
        gate_grad.astype(jnp.bfloat16)[None, None],
        up_grad.astype(jnp.bfloat16)[None, None],
        down_grad.astype(jnp.bfloat16)[None, None],
    )


def solution(mesh):
    sections, experts = mesh.devices.shape
    split = Mesh(
        mesh.devices.reshape(2, sections // 2, experts), ("half", "layer", "expert")
    )
    rows = P(("half", "layer"), "expert", None)
    weights = P(("half", "layer"), "expert", None, None)
    return jax.shard_map(
        per_device,
        mesh=split,
        in_specs=(rows, rows, rows, weights, weights, weights),
        out_specs=(rows, weights, weights, weights),
        check_vma=False,
    )
```

time: 852 us -> 324 us (0.38)
  the two profiles are of different devices: /device:TPU:158 before, /device:TPU:12 now
where the time goes in v1:
time: 324 us
  blocking collectives  206 us (64%)
  waiting for transfers between devices  93.7 us (29%)
  matrix products  16.5 us (5%)
  starting transfers between devices  4.01 us (1%)
    all_to_all x1, blocking collectives, per_device(): lax.all_to_all(send.reshape(peers, capacity, 2 * width), PAIR, split_axis...  206 us
    all_to_all x1, waiting for transfers between devices, per_device(): lax.all_to_all(back.reshape(peers, capacity, width), PAIR, split_axis=0,...  93.7 us
  transfers between devices with their start and end apart: 1, of which 1 were waited for; matrix products, arithmetic and copies ran while one was open for 2% of the time, Pallas kernels for 0%

profile of v1, /device:TPU:12, one launch (start us, length us, event | category | flops | bytes accessed | tf_op | source)
XLA Modules:
  0.0 323.6 jit_solution(15562565236229915704)
XLA Ops:
  0.6 0.0 copy-start
  0.7 0.8 fusion.29
  1.5 0.2 reduce_window_sum.11
  1.6 0.8 select_reduce_fusion
  2.5 0.7 multiply_add_fusion
  3.1 2.5 convolution_convert_fusion
  5.6 0.0 copy-start.3
  5.6 206.2 %all_to_all.10 = bf16[32,16,4096]{2,1,0:T(8,128)(2,1)S(1)} all-to-all(bf16[32,16,4096]{2,1,0:T(8,128)(2,1)S(1)} %bitcast.36), channel_id=1, replica_groups=mesh['half'=2,'layer'=16,'expert'=16] {'half','expert'}, dimensions={0} | all-to-all | bytes 8388608 | tf_op jit(solution)/shard_map/all_to_all | solution.py:30
  211.9 0.0 copy-start.1
  211.9 0.0 copy-start.4
  211.9 0.0 copy-done
  211.9 0.7 fusion.9
  212.6 0.0 copy-done.3
  212.6 0.7 fusion.11
  213.3 0.0 copy-done.4
  213.3 0.7 multiply_convert_fusion.1
  214.0 0.0 copy-done.1
  214.1 0.7 fusion.16
  214.8 2.0 add_convert_fusion
  216.8 4.0 %all-to-all-start.1 = ((bf16[32,16,2048]{2,1,0:T(8,128)(2,1)}), bf16[32,16,2048]{2,1,0:T(8,128)(2,1)S(1)}, u32[]{:S(2)}, u32[]{:S(2)}) async-start(bf16[32,16,2048]{2,1,0:T(8,128)(2,1)} %bitcast.38), calls=%async_computation.1 | async-start | bytes 4194304 | tf_op jit(solution)/shard_map/all_to_all | solution.py:51
  220.8 0.0 copy-start.2
  220.8 3.3 %fusion.2 = bf16[1,1,2048,128]{3,2,1,0:T(8,128)(2,1)} fusion(bf16[512,128]{1,0:T(8,128)(2,1)S(1)} %get-tuple-element.4, bf16[512,4096]{1,0:T(8,128)(2,1)} %bitcast.42), kind=kOutput, calls=%fused_computation.8 | convolution fusion | flops 268697600 | bytes 2752512 | tf_op jit(solution)/shard_map/dot_general | solution.py:60
  224.1 3.1 fusion.1
  227.3 0.0 copy-done.2
  227.3 1.3 fusion.3
  228.6 93.7 %all-to-all-done.1 = bf16[32,16,2048]{2,1,0:T(8,128)(2,1)S(1)} async-done(((bf16[32,16,2048]{2,1,0:T(8,128)(2,1)}), bf16[32,16,2048]{2,1,0:T(8,128)(2,1)S(1)}, u32[]{:S(2)}, u32[]{:S(2)}) %all-to-all-start.1) | async-done | bytes 2097184 | tf_op jit(solution)/shard_map/all_to_all | solution.py:51
  322.3 1.3 fusion
  (1 shorter events, 0.0 us)
Async XLA Ops:
  0.6 211.2 %copy-start = (bf16[1,1,2048,128]{3,2,1,0:T(8,128)(2,1)S(1)}, bf16[1,1,2048,128]{3,2,1,0:T(8,128)(2,1)}, u32[]{:S(2)}) copy-start(bf16[1,1,2048,128]{3,2,1,0:T(8,128)(2,1)} %param.9) | copy-start | bytes 1572868
  5.6 207.0 %copy-start.3 = (bf16[1,1,2048,128]{3,2,1,0:T(8,128)(2,1)S(1)}, bf16[1,1,2048,128]{3,2,1,0:T(8,128)(2,1)}, u32[]{:S(2)}) copy-start(bf16[1,1,2048,128]{3,2,1,0:T(8,128)(2,1)} %param.10) | copy-start | bytes 1572868
  211.9 2.2 copy-start.1
  211.9 1.5 copy-start.4
  216.8 105.4 %all-to-all-start.1 = ((bf16[32,16,2048]{2,1,0:T(8,128)(2,1)}), bf16[32,16,2048]{2,1,0:T(8,128)(2,1)S(1)}, u32[]{:S(2)}, u32[]{:S(2)}) async-start(bf16[32,16,2048]{2,1,0:T(8,128)(2,1)} %bitcast.38), calls=%async_computation.1 | async-start | bytes 4194304 | tf_op jit(solution)/shard_map/all_to_all | solution.py:51
  220.8 6.5 %copy-start.2 = (bf16[32,16,4096]{2,1,0:T(8,128)(2,1)S(1)}, bf16[32,16,4096]{2,1,0:T(8,128)(2,1)}, u32[]{:S(2)}) copy-start(bf16[32,16,4096]{2,1,0:T(8,128)(2,1)} %copy-done.1) | copy-start | bytes 12582916
